TPU v7x, 256 devices: a whole 4x4x8 slice. The times are simulated.
256 devices in a mesh: kv: 8 (over x, core), seq: 8 (over z), vocab: 4 (over y).
Axes of the slice: x: 4, y: 4, z: 8, core: 2. Of those that a mesh axis runs over, the one named last changes fastest.
Arguments:
- hidden_state: bfloat16 [48, 4, 3584], P('kv', 'vocab', 'seq'), may hold values from -6 to 6
- input_projection: bfloat16 [3584, 8, 1024], P('seq', 'kv'), may hold values from -0.09375 to 0.09375
- output_projection: bfloat16 [8, 512, 3584], P('kv', None, 'seq'), may hold values from -0.09375 to 0.09375
- norm_pre_attention: float32 [3584], P('seq'), may hold values from 0.1 to 1.9
- norm_post_attention: float32 [3584], P('seq'), may hold values from 0.1 to 1.9
- norm_pre_feedforward: float32 [3584], P('seq'), may hold values from 0.1 to 1.9
- norm_post_feedforward: float32 [3584], P('seq'), may hold values from 0.1 to 1.9
- norm_final: float32 [3584], P('seq'), may hold values from 0.1 to 1.9
- cache_keys: bfloat16 [4, 16384, 8, 256], P('vocab', 'seq', 'kv')
- cache_values: bfloat16 [4, 16384, 8, 256], P('vocab', 'seq', 'kv')
- cache_length: int32 [4], P('vocab'), may hold values from 1 to 16379, as said below
- ancestors: int32 [4, 48, 48], P('vocab'), may hold values from 0 to 1, as said below
- accepted_path: int32 [4, 5], P('vocab'), may hold values from 0 to 47, as said below
- gate_up_weight: bfloat16 [3584, 2, 14336], P('seq', None, ('kv', 'vocab')), may hold values from -0.09375 to 0.09375
- down_weight: bfloat16 [14336, 3584], P(('kv', 'vocab'), 'seq'), may hold values from -0.046875 to 0.046875
- draft_weight: bfloat16 [4, 3584, 3584], P(None, 'seq', ('kv', 'vocab')), may hold values from -0.09375 to 0.09375
- draft_bias: float32 [4, 3584], P(None, ('kv', 'vocab')), may hold values from -3 to 3
- vocab_weight: bfloat16 [131072, 3584], P(('kv', 'seq', 'vocab'))
- candidate_tokens: int32 [5, 48, 4, 8], replicated, may hold values from 0 to 131071
Outputs:
- keys_updated: bfloat16 [4, 16384, 8, 256], P('vocab', 'seq', 'kv')
- values_updated: bfloat16 [4, 16384, 8, 256], P('vocab', 'seq', 'kv')
- log_normalizer: float32 [5, 48, 4], replicated
- candidate_logits: float32 [5, 48, 4, 8], replicated
Inputs may be any that keep to these rules, and one draw needn't show every extreme that they name: The first cache_length[k] slots of tenant k's cache are filled; in every draw some tenant holds exactly 16379. ancestors[k, t, u] is 1 exactly when u is t or an ancestor of t in tenant k's tree; node 0 is the root and every parent has a lower index than its child. accepted_path[k] lists 5 nodes of tenant k's tree from the root down, each the parent of the next; the last of them is node 47.
All inputs are finite; a program needn't handle non-finite values.
Results may differ from a plain program's by a relative error of at most 0.02.
Values may be sent and summed in bfloat16 or wider, within the bound.
A program may use at most 64 MiB of HBM per device.

v0:
```python
import jax
import jax.numpy as jnp
from jax import lax
from jax.sharding import PartitionSpec as P

MODEL_WIDTH = 3584
HEAD_SIZE = 256
CAND = 8
EPSILON = 1e-06
SCORE_CAP = 50.0
LOGIT_CAP = 30.0


def apply_rotary(vectors, token_positions):
    half_dim = vectors.shape[-1] // 2
    frequency = 10000.0 ** (-2.0 * jnp.arange(half_dim, dtype=jnp.float32) / vectors.shape[-1])
    angles = token_positions.astype(jnp.float32)[..., None] * frequency
    cosine = jnp.cos(angles)
    sine_part = jnp.sin(angles)
    first_half = vectors[..., :half_dim]
    second_half = vectors[..., half_dim:]
    return jnp.concatenate(
        [
            first_half * cosine - second_half * sine_part,
            second_half * cosine + first_half * sine_part,
        ],
        axis=-1,
    )


def capped_weight(scores):
    return jnp.exp(SCORE_CAP * jnp.tanh(scores * 0.0625 / SCORE_CAP))


def row_inverse(values):
    totals = lax.psum(jnp.sum(values * values, axis=-1), "seq")
    return lax.rsqrt(totals / MODEL_WIDTH + EPSILON)[:, None]


def gated_units(gate_up, squares):
    inverse = lax.rsqrt(squares / MODEL_WIDTH + EPSILON)[:, None]
    return (
        jax.nn.gelu(gate_up[:, 0] * inverse, approximate=True) * (gate_up[:, 1] * inverse)
    ).astype(jnp.bfloat16)


def local(
    hidden_state,
    input_projection,
    output_projection,
    norm_pre_attention,
    norm_post_attention,
    norm_pre_feedforward,
    norm_post_feedforward,
    norm_final,
    cache_keys,
    cache_values,
    cache_length,
    ancestors,
    accepted_path,
    gate_up_weight,
    down_weight,
    draft_weight,
    draft_bias,
    vocab_weight,
    candidate_tokens,
):
    tok_block = hidden_state.shape[0]
    kv_count = lax.axis_size("kv")
    tenants = lax.axis_size("vocab")
    tree_size = tok_block * kv_count
    own_state = hidden_state[:, 0, :]
    tenant_state = lax.all_gather(own_state, "kv", axis=0, tiled=True)
    tenant_float = tenant_state.astype(jnp.float32)
    scaled_input = (tenant_float * norm_pre_attention).astype(jnp.bfloat16)
    projected_rows = jnp.einsum(
        "td,dhc->thc", scaled_input, input_projection, preferred_element_type=jnp.float32
    )
    projected_rows, squares = lax.psum(
        (projected_rows, jnp.sum(tenant_float * tenant_float, axis=-1)), "seq"
    )
    projected_rows = projected_rows * lax.rsqrt(squares / MODEL_WIDTH + EPSILON)[:, None, None]
    head_count = projected_rows.shape[1]
    depths = jnp.sum(ancestors[0], axis=-1) - 1
    length = cache_length[0]
    token_positions = length + depths
    query_rows = apply_rotary(
        projected_rows[:, :, : 2 * HEAD_SIZE].reshape(tree_size, head_count, 2, HEAD_SIZE),
        token_positions[:, None, None],
    ).astype(jnp.bfloat16)
    new_keys = apply_rotary(
        projected_rows[:, :, 2 * HEAD_SIZE : 3 * HEAD_SIZE], token_positions[:, None]
    ).astype(jnp.bfloat16)
    new_values = projected_rows[:, :, 3 * HEAD_SIZE :].astype(jnp.bfloat16)
    block_size = cache_keys.shape[1]
    block_start = lax.axis_index("seq") * block_size
    cache_cells = block_start + jnp.arange(block_size, dtype=jnp.int32)
    scores = jnp.einsum(
        "thgc,shc->thgs", query_rows, cache_keys[0], preferred_element_type=jnp.float32
    )
    weights = jnp.where((cache_cells < length)[None, None, None, :], capped_weight(scores), 0.0)
    numerator = jnp.einsum(
        "thgs,shc->thgc",
        weights.astype(jnp.bfloat16),
        cache_values[0],
        preferred_element_type=jnp.float32,
    )
    numerator, denominator = lax.psum((numerator, jnp.sum(weights, axis=-1)), "seq")
    tree_scores = jnp.einsum(
        "thgc,uhc->thgu", query_rows, new_keys, preferred_element_type=jnp.float32
    )
    tree_weights = jnp.where(ancestors[0][:, None, None, :] > 0, capped_weight(tree_scores), 0.0)
    numerator = numerator + jnp.einsum(
        "thgu,uhc->thgc",
        tree_weights.astype(jnp.bfloat16),
        new_values,
        preferred_element_type=jnp.float32,
    )
    denominator = denominator + jnp.sum(tree_weights, axis=-1)
    attended = (
        (numerator / denominator[..., None])
        .astype(jnp.bfloat16)
        .reshape(tree_size, head_count * 2 * HEAD_SIZE)
    )
    out_matrix = output_projection.reshape(head_count * 2 * HEAD_SIZE, output_projection.shape[2])
    attention_out = lax.psum_scatter(
        jnp.dot(attended, out_matrix, preferred_element_type=jnp.float32),
        "kv",
        scatter_dimension=0,
        tiled=True,
    )
    first_sum = (
        own_state.astype(jnp.float32)
        + attention_out * row_inverse(attention_out) * norm_post_attention
    ).astype(jnp.bfloat16)
    all_state = lax.all_gather(first_sum, ("kv", "vocab"), axis=0, tiled=True)
    all_float = all_state.astype(jnp.float32)
    scaled_ffn = (all_float * norm_pre_feedforward).astype(jnp.bfloat16)
    gate_up = jnp.einsum(
        "td,dcf->tcf", scaled_ffn, gate_up_weight, preferred_element_type=jnp.float32
    )
    ffn_squares = jnp.sum(all_float * all_float, axis=-1)
    gate_up, ffn_squares = lax.psum((gate_up, ffn_squares), "seq")
    activated = gated_units(gate_up, ffn_squares)
    ffn_out = lax.psum_scatter(
        jnp.dot(activated, down_weight, preferred_element_type=jnp.float32),
        ("kv", "vocab"),
        scatter_dimension=0,
        tiled=True,
    )
    first_float = first_sum.astype(jnp.float32)
    second_sum = (first_float + ffn_out * row_inverse(ffn_out) * norm_post_feedforward).astype(
        jnp.bfloat16
    )
    second_float = second_sum.astype(jnp.float32)
    normed = (second_float * row_inverse(second_float) * norm_final).astype(jnp.bfloat16)
    gathered = lax.all_gather(normed, ("kv", "vocab"), axis=0, tiled=True)
    lifted = jnp.einsum("td,ndc->tnc", gathered, draft_weight, preferred_element_type=jnp.float32)
    lifted = lax.psum(lifted.astype(jnp.bfloat16), "seq").astype(jnp.float32)
    branch = jax.nn.silu(lifted + draft_bias).astype(jnp.bfloat16)
    row_count = gathered.shape[0]
    vocab_rows = vocab_weight.shape[0]
    draft_count = branch.shape[1]
    columns = vocab_weight
    base_logits = lax.dot_general(
        lax.all_gather(gathered, "seq", axis=1, tiled=True),
        columns,
        (((1,), (1,)), ((), ())),
        preferred_element_type=jnp.float32,
    )
    columns = vocab_weight
    draft_extra = jnp.einsum(
        "tnc,vc->tnv",
        lax.all_gather(branch, ("kv", "vocab"), axis=2, tiled=True),
        columns,
        preferred_element_type=jnp.float32,
    )
    raw_logits = jnp.concatenate(
        [base_logits[:, None, :], base_logits[:, None, :] + draft_extra], axis=1
    )
    logits = LOGIT_CAP * jnp.tanh(raw_logits / LOGIT_CAP)
    totals = jnp.sum(jnp.exp(logits), axis=-1)
    head_total = draft_count + 1
    candidates = candidate_tokens.reshape(head_total, kv_count, tok_block, tenants, CAND)
    candidates = jnp.transpose(candidates, (0, 1, 3, 2, 4)).reshape(head_total, row_count, CAND)
    candidates = jnp.transpose(candidates, (1, 0, 2))
    vocab_start = lax.axis_index(("kv", "seq", "vocab")) * vocab_rows
    local_tokens = candidates - vocab_start
    entry_index = jnp.arange(vocab_rows, dtype=jnp.int32)
    picked = jnp.stack(
        [
            jnp.sum(
                jnp.where(entry_index == local_tokens[:, :, column : column + 1], logits, 0.0),
                axis=-1,
            )
            for column in range(CAND)
        ],
        axis=-1,
    )
    totals, picked = lax.psum((totals, picked), ("kv", "seq", "vocab"))
    log_totals = jnp.transpose(jnp.log(totals)).reshape(head_total, kv_count, tenants, tok_block)
    log_normalizer = jnp.transpose(log_totals, (0, 1, 3, 2)).reshape(head_total, tree_size, tenants)
    picked = jnp.transpose(picked, (1, 0, 2)).reshape(
        head_total, kv_count, tenants, tok_block, CAND
    )
    candidate_logits = jnp.transpose(picked, (0, 1, 3, 2, 4)).reshape(
        head_total, tree_size, tenants, CAND
    )
    accept_count = accepted_path.shape[1]
    slot_rows = length + jnp.arange(accept_count, dtype=jnp.int32)
    tree_nodes = jnp.arange(tree_size, dtype=jnp.int32)
    matches = (cache_cells[:, None, None] == slot_rows[None, :, None]) & (
        accepted_path[0][None, :, None] == tree_nodes[None, None, :]
    )
    selector = jnp.sum(matches.astype(jnp.float32), axis=1)
    written = jnp.sum(selector, axis=-1) > 0.0
    selector = selector.astype(jnp.bfloat16)

    def write_path(old_block, fresh_rows):
        moved_rows = jnp.dot(
            selector, fresh_rows.reshape(tree_size, -1), preferred_element_type=jnp.float32
        ).astype(jnp.bfloat16)
        return jnp.where(
            written[:, None], moved_rows, old_block[0].reshape(block_size, -1)
        ).reshape(old_block.shape)

    keys_updated = write_path(cache_keys, new_keys)
    values_updated = write_path(cache_values, new_values)
    return (keys_updated, values_updated, log_normalizer, candidate_logits)


def solution(mesh):
    placed = (
        P("kv", "vocab", "seq"),
        P("seq", "kv", None),
        P("kv", None, "seq"),
        P("seq"),
        P("seq"),
        P("seq"),
        P("seq"),
        P("seq"),
        P("vocab", "seq", "kv", None),
        P("vocab", "seq", "kv", None),
        P("vocab"),
        P("vocab", None, None),
        P("vocab", None),
        P("seq", None, ("kv", "vocab")),
        P(("kv", "vocab"), "seq"),
        P(None, "seq", ("kv", "vocab")),
        P(None, ("kv", "vocab")),
        P(("kv", "seq", "vocab"), None),
        P(),
    )
    return jax.shard_map(
        local,
        mesh=mesh,
        in_specs=placed,
        out_specs=(P("vocab", "seq", "kv", None), P("vocab", "seq", "kv", None), P(), P()),
        check_vma=False,
    )
```

profile of v0, /device:TPU:1, one launch (start us, length us, event | category | flops | bytes accessed | tf_op | source)
XLA Modules:
  0.0 775.7 jit_solution(17245792410160348582)
XLA Ops:
  8.1 15.8 %all-gather = bf16[48,1,448]{2,1,0:T(2,128)(2,1)S(1)} all-gather(bf16[6,1,448]{2,1,0:T(2,128)(2,1)S(1)} %copy.52), channel_id=2, replica_groups=mesh['kv'=8,'seq'=8,'vocab'=4] {'kv'}, dimensions={0}, use_global_device_ids=true | all-gather | bytes 48384 | tf_op jit(solution)/shard_map/all_gather | solution.py:73
  24.0 2.2 convolution_bitcast_fusion
  26.3 15.0 %psum.85 = f32[48]{0:T(128)S(1)} all-reduce(f32[48]{0:T(128)S(1)} %fusion.56), channel_id=1, replica_groups=mesh['kv'=8,'seq'=8,'vocab'=4] {'seq'}, use_global_device_ids=true, to_apply=%region_4.5 | all-reduce | flops 48 | bytes 384 | tf_op jit(solution)/shard_map/psum | solution.py:79
  43.9 50.6 %all-reduce.10.cloned.1.call-done = f32[48,1,1024]{2,0,1:T(8,128)} async-done(((f32[48,1,1024]{2,0,1:T(8,128)}), f32[48,1,1024]{2,0,1:T(8,128)}) %all-reduce.10.cloned.1.call-update) | async-done | bytes 196624 | tf_op jit(solution)/shard_map/psum | solution.py:79
  97.1 12.7 %psum.87 = f32[48,1,2]{0,2,1:T(2,128)S(1)} all-reduce(f32[48,1,2]{0,2,1:T(2,128)S(1)} %bitcast.224), channel_id=1, replica_groups=mesh['kv'=8,'seq'=8,'vocab'=4] {'seq'}, use_global_device_ids=true, to_apply=%region_8.9 | all-reduce | flops 96 | bytes 768 | tf_op jit(solution)/shard_map/psum | solution.py:108
  109.8 2.0 convolution_bitcast_fusion.1
  112.0 73.8 %all-reduce.12.cloned.1.call-done = f32[48,1,2,256]{3,0,2,1:T(8,128)} async-done(((f32[48,1,2,256]{3,0,2,1:T(8,128)}), f32[48,1,2,256]{3,0,2,1:T(8,128)}) %all-reduce.12.cloned.1.call-update) | async-done | bytes 98320 | tf_op jit(solution)/shard_map/psum | solution.py:108
  187.3 18.1 %fusion = f32[8,448]{1,0:T(8,128)S(1)} fusion(f32[48,448]{1,0:T(8,128)S(1)} %fusion.35), kind=kCustom, calls=%all-reduce-scatter | all-reduce-scatter fusion | flops 28673 | bytes 101376
  205.3 3.4 collective-permute-start
  212.0 11.6 %psum.88 = f32[6]{0:T(128)S(1)} all-reduce(f32[6]{0:T(128)S(1)} %multiply_reduce_fusion.2), channel_id=1, replica_groups=mesh['kv'=8,'seq'=8,'vocab'=4] {'seq'}, use_global_device_ids=true, to_apply=%region_12.13 | all-reduce | flops 6 | bytes 48 | tf_op jit(solution)/shard_map/psum | solution.py:36
  223.7 45.5 %all-gather.1 = bf16[32,6,448]{2,1,0:T(8,128)(2,1)S(1)} all-gather(bf16[1,6,448]{2,1,0:T(8,128)(2,1)S(1)} %bitcast.223), channel_id=1, replica_groups=mesh['kv'=8,'seq'=8,'vocab'=4] {'kv','vocab'}, dimensions={0}, use_global_device_ids=true | all-gather | bytes 177408 | tf_op jit(solution)/shard_map/all_gather | solution.py:136
  270.8 11.5 %psum.90 = f32[192]{0:T(256)S(1)} all-reduce(f32[192]{0:T(256)S(1)} %multiply_reduce_fusion), channel_id=1, replica_groups=mesh['kv'=8,'seq'=8,'vocab'=4] {'seq'}, use_global_device_ids=true, to_apply=%region_15.16 | all-reduce | flops 192 | bytes 1536 | tf_op jit(solution)/shard_map/psum | solution.py:143
  282.3 57.1 %all-reduce.14.cloned.1.call-done = f32[192,2,448]{2,0,1:T(8,128)} async-done(((f32[192,2,448]{2,0,1:T(8,128)}), f32[192,2,448]{2,0,1:T(8,128)}) %all-reduce.14.cloned.1.call-update) | async-done | bytes 688144 | tf_op jit(solution)/shard_map/psum | solution.py:143
  341.1 68.1 %fusion.1 = f32[8,448]{1,0:T(8,128)S(1)} fusion(f32[192,448]{1,0:T(8,128)S(1)} %fusion.53), kind=kCustom, calls=%all-reduce-scatter.1 | all-reduce-scatter fusion | flops 114689 | bytes 359424
  411.1 1.9 collective-permute-start.3
  414.4 1.9 collective-permute-start.4
  418.3 5.9 collective-permute-start.6
  424.2 6.8 collective-permute-start.7
  431.0 3.9 collective-permute-start.8
  437.2 12.6 %psum.91 = f32[6]{0:T(128)S(1)} all-reduce(f32[6]{0:T(128)S(1)} %multiply_reduce_fusion.1), channel_id=1, replica_groups=mesh['kv'=8,'seq'=8,'vocab'=4] {'seq'}, use_global_device_ids=true, to_apply=%region_18.19 | all-reduce | flops 6 | bytes 48 | tf_op jit(solution)/shard_map/psum | solution.py:36
  450.0 10.7 %psum.92 = f32[6]{0:T(128)S(1)} all-reduce(f32[6]{0:T(128)S(1)} %get-tuple-element.17), channel_id=1, replica_groups=mesh['kv'=8,'seq'=8,'vocab'=4] {'seq'}, use_global_device_ids=true, to_apply=%region_20.21 | all-reduce | flops 6 | bytes 48 | tf_op jit(solution)/shard_map/psum | solution.py:36
  460.8 48.2 %all-gather.2 = bf16[32,6,448]{2,1,0:T(8,128)(2,1)S(1)} all-gather(bf16[1,6,448]{2,1,0:T(8,128)(2,1)S(1)} %fusion.82), channel_id=1, replica_groups=mesh['kv'=8,'seq'=8,'vocab'=4] {'kv','vocab'}, dimensions={0}, use_global_device_ids=true | all-gather | bytes 177408 | tf_op jit(solution)/shard_map/all_gather | solution.py:157
  511.2 64.1 %all-reduce.16.cloned.1.call-done = bf16[192,4,112]{2,0,1:T(8,128)(2,1)} async-done(((bf16[192,4,112]{2,0,1:T(8,128)(2,1)}), bf16[192,4,112]{2,0,1:T(8,128)(2,1)}) %all-reduce.16.cloned.1.call-update) | async-done | bytes 172048 | tf_op jit(solution)/shard_map/psum | solution.py:159
  581.5 2.5 fusion.6
  585.5 30.5 %all-gather.9.cloned.1.call-done = bf16[8,448,192]{1,2,0:T(8,128)(2,1)} async-done(((bf16[1,448,192]{1,2,0:T(8,128)(2,1)}), bf16[8,448,192]{1,2,0:T(8,128)(2,1)}) %all-gather.9.cloned.1.call-update) | async-done | bytes 1376272 | tf_op jit(solution)/shard_map/all_gather | solution.py:166
  616.1 2.3 copy.59
  618.4 2.7 reshape.412
  621.1 3.8 fusion.95
  625.0 52.4 %all-gather.7.cloned.1.call-done = bf16[192,4,3584]{0,1,2:T(4,128)(2,1)} async-done(((bf16[192,4,112]{0,1,2:T(4,128)(2,1)}), bf16[192,4,3584]{0,1,2:T(4,128)(2,1)}) %all-gather.7.cloned.1.call-update) | async-done | bytes 5505040 | tf_op jit(solution)/shard_map/all_gather | solution.py:174
  677.3 8.2 %fusion.17 = f32[192,4,512]{2,0,1:T(8,128)S(1)} fusion(bf16[512,3584]{1,0:T(8,128)(2,1)} %param.36, bf16[192,4,3584]{0,1,2:T(4,128)(2,1)} %all-gather.7.cloned.1.call-done, f32[192,512]{1,0:T(8,128)S(1)} %fusion.95), kind=kOutput, calls=%fused_computation.38 | convolution fusion | flops 2818965504 | bytes 11141120 | tf_op jit(solution)/shard_map/tnc,vc->tnv/dot_general | solution.py:172
  685.6 4.4 select_reduce_fusion
  691.4 76.6 %all-reduce.4 = (f32[192,5]{0,1:T(8,128)S(1)}, f32[5,48,4,8]{1,3,2,0:T(8,128)}) all-reduce(f32[192,5]{0,1:T(8,128)S(1)} %get-tuple-element.19, f32[5,48,4,8]{1,3,2,0:T(8,128)S(1)} %reshape.401), channel_id=1, replica_groups=mesh['kv'=8,'seq'=8,'vocab'=4] {'kv','seq','vocab'}, use_global_device_ids=true, to_apply=%region_23.24 | all-reduce | flops 8640 | bytes 69120 | tf_op jit(solution)/shard_map/psum | solution.py:200
  (150 shorter events, 32.0 us)
Async XLA Ops:
  7.2 262.2 %copy-start = (bf16[448,2,448]{2,1,0:T(2,128)(2,1)S(1)}, bf16[448,2,448]{2,1,0:T(2,128)(2,1)}, u32[]{:S(2)}) copy-start(bf16[448,2,448]{2,1,0:T(2,128)(2,1)} %param.32) | copy-start | bytes 2408452
  7.2 88.7 %copy-start.2 = (bf16[1,2048,1,256]{3,1,2,0:T(8,128)(2,1)S(1)}, bf16[1,2048,1,256]{3,1,2,0:T(8,128)(2,1)}, u32[]{:S(2)}) copy-start(bf16[1,2048,1,256]{3,1,2,0:T(8,128)(2,1)} %param.27) | copy-start | bytes 3145732
  7.2 87.3 %all-reduce.10.cloned.1.call-start = ((), (), s32[]{:S(2)}) async-start(), calls=%async_computation | async-start | bytes 393216 | tf_op jit(solution)/shard_map/psum | solution.py:79
  26.1 83.6 %copy-start.1 = (bf16[1,2048,1,256]{3,1,2,0:T(8,128)(2,1)S(1)}, bf16[1,2048,1,256]{3,1,2,0:T(8,128)(2,1)}, u32[]{:S(2)}) copy-start(bf16[1,2048,1,256]{3,1,2,0:T(8,128)(2,1)} %param.28) | copy-start | bytes 3145732
  26.2 159.7 %all-reduce.12.cloned.1.call-start = ((), (), s32[]{:S(2)}) async-start(), calls=%async_computation.1 | async-start | bytes 196608 | tf_op jit(solution)/shard_map/psum | solution.py:108
  97.1 89.9 %copy-start.3 = (bf16[1,512,448]{1,2,0:T(8,128)(2,1)S(1)}, bf16[1,512,448]{1,2,0:T(8,128)(2,1)}, u32[]{:S(2)}) copy-start(bf16[1,512,448]{1,2,0:T(8,128)(2,1)} %param.21) | copy-start | bytes 1376260
  97.1 113.3 %copy-start.20 = (u32[256]{0:T(256)S(1)}, u32[256]{0:T(256)}, u32[]{:S(2)}) copy-start(u32[256]{0:T(256)} %constant.87) | copy-start | bytes 3076
  97.1 126.5 %copy-start.13 = (bf16[6,1,448]{2,0,1:T(8,128)(2,1)S(1)}, bf16[6,1,448]{2,0,1:T(8,128)(2,1)}, u32[]{:S(2)}) copy-start(bf16[6,1,448]{2,0,1:T(8,128)(2,1)} %param.19) | copy-start | bytes 16132
  97.1 126.5 %copy-start.16 = (f32[448]{0:T(512)S(1)}, f32[448]{0:T(512)}, u32[]{:S(2)}) copy-start(f32[448]{0:T(512)} %param.23) | copy-start | bytes 5380
  109.8 159.6 %copy-start.14 = (f32[448]{0:T(512)S(1)}, f32[448]{0:T(512)}, u32[]{:S(2)}) copy-start(f32[448]{0:T(512)} %param.24) | copy-start | bytes 5380
  111.8 227.7 %all-reduce.14.cloned.1.call-start = ((), (), s32[]{:S(2)}) async-start(), calls=%async_computation.2 | async-start | bytes 1572864 | tf_op jit(solution)/shard_map/psum | solution.py:143
  205.3 6.3 collective-permute-start
  208.8 2.8 collective-permute-start.1
  270.6 164.4 %copy-start.19 = (u32[256]{0:T(256)S(1)}, u32[256]{0:T(256)}, u32[]{:S(2)}) copy-start(u32[256]{0:T(256)} %constant.91) | copy-start | bytes 3076
  270.6 179.2 %copy-start.17 = (f32[448]{0:T(512)S(1)}, f32[448]{0:T(512)}, u32[]{:S(2)}) copy-start(f32[448]{0:T(512)} %param.25) | copy-start | bytes 5380
  270.6 190.1 %copy-start.18 = (f32[448]{0:T(512)S(1)}, f32[448]{0:T(512)}, u32[]{:S(2)}) copy-start(f32[448]{0:T(512)} %param.26) | copy-start | bytes 5380
  270.6 238.5 %copy-start.4 = (bf16[4,448,112]{2,1,0:T(8,128)(2,1)S(1)}, bf16[4,448,112]{2,1,0:T(8,128)(2,1)}, u32[]{:S(2)}) copy-start(bf16[4,448,112]{2,1,0:T(8,128)(2,1)} %param.34) | copy-start | bytes 1204228
  270.7 304.6 %all-reduce.16.cloned.1.call-start = ((), (), s32[]{:S(2)}) async-start(), calls=%async_computation.3 | async-start | bytes 393216 | tf_op jit(solution)/shard_map/psum | solution.py:159
  341.1 234.2 %copy-start.15 = (f32[4,112]{1,0:T(4,128)S(1)}, f32[4,112]{1,0:T(4,128)}, u32[]{:S(2)}) copy-start(f32[4,112]{1,0:T(4,128)} %param.35) | copy-start | bytes 5380
  409.1 15.1 %collective-permute-start.2 = (f32[8,448]{1,0:T(8,128)S(1)}, f32[8,448]{1,0:T(8,128)S(1)}, u32[]{:S(2)}, u32[]{:S(2)}) collective-permute-start(f32[8,448]{1,0:T(8,128)S(1)} %fusion.1), channel_id=1, source_target_pairs={{0,1},{1,2},{2,3},{3,32},{32,33},{33,34},{34,35},{35,64},{64,65},{... | collective-permute-start | bytes 43016
  411.1 20.0 %collective-permute-start.3 = (f32[8,448]{1,0:T(8,128)S(1)}, f32[8,448]{1,0:T(8,128)S(1)}, u32[]{:S(2)}, u32[]{:S(2)}) collective-permute-start(f32[8,448]{1,0:T(8,128)S(1)} %fusion.1), channel_id=1, source_target_pairs={{0,2},{1,3},{2,32},{3,33},{32,34},{33,35},{34,64},{35,65},{64,66},... | collective-permute-start | bytes 43016
  413.0 164.3 %copy-start.5 = (s32[5,48,4,8]{1,3,2,0:T(8,128)S(1)}, s32[5,48,4,8]{1,3,2,0:T(8,128)}, u32[]{:S(2)}) copy-start(s32[5,48,4,8]{1,3,2,0:T(8,128)} %param.37) | copy-start | bytes 92164
  413.0 5.3 collective-permute-start.9
  414.4 21.8 %collective-permute-start.4 = (f32[8,448]{1,0:T(8,128)S(1)}, f32[8,448]{1,0:T(8,128)S(1)}, u32[]{:S(2)}, u32[]{:S(2)}) collective-permute-start(f32[8,448]{1,0:T(8,128)S(1)} %fusion.1), channel_id=1, source_target_pairs={{0,3},{1,32},{2,33},{3,34},{32,35},{33,64},{34,65},{35,66},{64,67}... | collective-permute-start | bytes 43016
  416.4 19.9 %collective-permute-start.5 = (f32[8,448]{1,0:T(8,128)S(1)}, f32[8,448]{1,0:T(8,128)S(1)}, u32[]{:S(2)}, u32[]{:S(2)}) collective-permute-start(f32[8,448]{1,0:T(8,128)S(1)} %fusion.1), channel_id=1, source_target_pairs={{0,32},{1,33},{2,34},{3,35},{32,64},{33,65},{34,66},{35,67},{64,96... | collective-permute-start | bytes 43016
  418.3 17.9 %collective-permute-start.6 = (f32[8,448]{1,0:T(8,128)S(1)}, f32[8,448]{1,0:T(8,128)S(1)}, u32[]{:S(2)}, u32[]{:S(2)}) collective-permute-start(f32[8,448]{1,0:T(8,128)S(1)} %fusion.1), channel_id=1, source_target_pairs={{0,33},{1,34},{2,35},{3,64},{32,65},{33,66},{34,67},{35,96},{64,97... | collective-permute-start | bytes 43016
  424.2 12.1 %collective-permute-start.7 = (f32[8,448]{1,0:T(8,128)S(1)}, f32[8,448]{1,0:T(8,128)S(1)}, u32[]{:S(2)}, u32[]{:S(2)}) collective-permute-start(f32[8,448]{1,0:T(8,128)S(1)} %fusion.1), channel_id=1, source_target_pairs={{0,34},{1,35},{2,64},{3,65},{32,66},{33,67},{34,96},{35,97},{64,98... | collective-permute-start | bytes 43016
  431.0 5.2 collective-permute-start.8
  510.1 106.0 %all-gather.9.cloned.1.call-start = ((), (), s32[]{:S(2)}) async-start(), calls=%async_computation.5 | async-start | bytes 1769472 | tf_op jit(solution)/shard_map/all_gather | solution.py:166
  511.0 67.6 %copy-start.21 = (s32[1,5]{1,0:T(1,128)S(1)}, s32[1,5]{1,0:T(1,128)}, u32[]{:S(2)}) copy-start(s32[1,5]{1,0:T(1,128)} %param.31) | copy-start | bytes 64
  511.0 166.3 %all-gather.7.cloned.1.call-start = ((), (), s32[]{:S(2)}) async-start(), calls=%async_computation.4 | async-start | bytes 7569408 | tf_op jit(solution)/shard_map/all_gather | solution.py:174
  624.9 60.7 %copy-start.6 = (s32[192,5]{0,1:T(8,128)S(1)}, s32[192,5]{0,1:T(8,128)}, u32[]{:S(2)}) copy-start(s32[192,5]{0,1:T(8,128)} %get-tuple-element.43) | copy-start | bytes 11524
  (6 other events, 364.0 us)
Sparse Core Ops, SparseCore 0:
  26.3 68.1 all-reduce.9
  111.9 73.9 all-reduce.11
  270.8 68.6 all-reduce.13
  510.2 65.0 all-reduce.15
  576.9 39.1 all-gather.8
  618.5 58.7 all-gather.6
where the time goes:
time: 777 us; the launch traced here: 776 us
  blocking collectives  346 us (45%)
  waiting for transfers between devices  329 us (42%)
  starting transfers between devices  31.2 us (4%)
  matrix products  26.7 us (3%)
  between operations  16.9 us (2%)
  local copies, waits for them, and re-layouts  16 us (2%)
  other arithmetic  9.93 us (1%)
    unnamed x2, blocking collectives  86.2 us
    psum x1, blocking collectives, local(): totals, picked = lax.psum((totals, picked), ('kv', 'seq', 'vocab'))  76.6 us
    psum x1, waiting for transfers between devices, local(): lax.psum((numerator, jnp.sum(weights, axis=-1)), 'seq')  73.8 us
    psum x1, waiting for transfers between devices, local(): lifted = lax.psum(lifted.astype(jnp.bfloat16), 'seq').astype(jnp.float32)  64.1 us
    psum x1, waiting for transfers between devices, local(): gate_up, ffn_squares = lax.psum((gate_up, ffn_squares), 'seq')  57.1 us
    all_gather x1, waiting for transfers between devices, local(): lax.all_gather(branch, ('kv', 'vocab'), axis=2, tiled=True)  52.4 us
    psum x1, waiting for transfers between devices, local(): lax.psum((projected_rows, jnp.sum(tenant_float * tenant_float, axis=-1)),...  50.6 us
    all_gather x1, blocking collectives, local(): gathered = lax.all_gather(normed, ('kv', 'vocab'), axis=0, tiled=True)  48.2 us
  transfers between devices with their start and end apart: 16, of which 6 were waited for; matrix products, arithmetic and copies ran while one was open for 3% of the time, Pallas kernels for 0%

commit v1 on v0

--- a/solution.py
+++ b/solution.py
@@ -133,7 +133,12 @@
         own_state.astype(jnp.float32)
         + attention_out * row_inverse(attention_out) * norm_post_attention
     ).astype(jnp.bfloat16)
-    all_state = lax.all_gather(first_sum, ("kv", "vocab"), axis=0, tiled=True)
+    all_state = jnp.concatenate(
+        lax.all_to_all(
+            jnp.stack([first_sum] * lax.axis_size(("kv", "vocab"))), ("kv", "vocab"), 0, 0
+        ),
+        axis=0,
+    )
     all_float = all_state.astype(jnp.float32)
     scaled_ffn = (all_float * norm_pre_feedforward).astype(jnp.bfloat16)
     gate_up = jnp.einsum(

time: 777 us -> 749 us (0.964)
  blocking collectives: 346 us -> 322 us
    all_gather x1 -> x0, blocking collectives: 45.5 us -> none  [local(): all_state = lax.all_gather(first_sum, ('kv', 'vocab'), axis=0, tiled=True)]
    all_to_all x0 -> x1, blocking collectives: none -> 20.5 us  [local(): lax.all_to_all(jnp.stack([first_sum] * lax.axis_size(('kv', 'vocab'))), (...]
where the time goes in v1:
time: 749 us; the launch traced here: 748 us
  waiting for transfers between devices  325 us (43%)
  blocking collectives  322 us (43%)
  starting transfers between devices  31.2 us (4%)
  matrix products  26.7 us (4%)
  between operations  16.9 us (2%)
  local copies, waits for them, and re-layouts  16.2 us (2%)
  other arithmetic  9.97 us (1%)
    unnamed x2, blocking collectives  86.2 us
    psum x1, blocking collectives, local(): totals, picked = lax.psum((totals, picked), ('kv', 'seq', 'vocab'))  76.6 us
    psum x1, waiting for transfers between devices, local(): lax.psum((numerator, jnp.sum(weights, axis=-1)), 'seq')  73.8 us
    psum x1, waiting for transfers between devices, local(): lifted = lax.psum(lifted.astype(jnp.bfloat16), 'seq').astype(jnp.float32)  64.1 us
    psum x1, waiting for transfers between devices, local(): gate_up, ffn_squares = lax.psum((gate_up, ffn_squares), 'seq')  53.8 us
    all_gather x1, waiting for transfers between devices, local(): lax.all_gather(branch, ('kv', 'vocab'), axis=2, tiled=True)  52.4 us
    psum x1, waiting for transfers between devices, local(): lax.psum((projected_rows, jnp.sum(tenant_float * tenant_float, axis=-1)),...  50.6 us
    all_gather x1, blocking collectives, local(): gathered = lax.all_gather(normed, ('kv', 'vocab'), axis=0, tiled=True)  48.2 us
  transfers between devices with their start and end apart: 16, of which 6 were waited for; matrix products, arithmetic and copies ran while one was open for 3% of the time, Pallas kernels for 0%

profile of v1, /device:TPU:1, one launch (start us, length us, event | category | flops | bytes accessed | tf_op | source)
XLA Modules:
  0.0 747.9 jit_solution(12145641892386098343)
XLA Ops:
  8.1 15.8 %all-gather = bf16[48,1,448]{2,1,0:T(2,128)(2,1)S(1)} all-gather(bf16[6,1,448]{2,1,0:T(2,128)(2,1)S(1)} %copy.52), channel_id=2, replica_groups=mesh['kv'=8,'seq'=8,'vocab'=4] {'kv'}, dimensions={0}, use_global_device_ids=true | all-gather | bytes 48384 | tf_op jit(solution)/shard_map/all_gather | solution.py:73
  24.0 2.2 convolution_bitcast_fusion
  26.3 15.0 %psum.85 = f32[48]{0:T(128)S(1)} all-reduce(f32[48]{0:T(128)S(1)} %fusion.56), channel_id=1, replica_groups=mesh['kv'=8,'seq'=8,'vocab'=4] {'seq'}, use_global_device_ids=true, to_apply=%region_4.5 | all-reduce | flops 48 | bytes 384 | tf_op jit(solution)/shard_map/psum | solution.py:79
  43.9 50.6 %all-reduce.10.cloned.1.call-done = f32[48,1,1024]{2,0,1:T(8,128)} async-done(((f32[48,1,1024]{2,0,1:T(8,128)}), f32[48,1,1024]{2,0,1:T(8,128)}) %all-reduce.10.cloned.1.call-update) | async-done | bytes 196624 | tf_op jit(solution)/shard_map/psum | solution.py:79
  97.1 12.7 %psum.87 = f32[48,1,2]{0,2,1:T(2,128)S(1)} all-reduce(f32[48,1,2]{0,2,1:T(2,128)S(1)} %bitcast.222), channel_id=1, replica_groups=mesh['kv'=8,'seq'=8,'vocab'=4] {'seq'}, use_global_device_ids=true, to_apply=%region_8.9 | all-reduce | flops 96 | bytes 768 | tf_op jit(solution)/shard_map/psum | solution.py:108
  109.8 1.9 convolution_bitcast_fusion.1
  112.0 73.8 %all-reduce.12.cloned.1.call-done = f32[48,1,2,256]{3,0,2,1:T(8,128)} async-done(((f32[48,1,2,256]{3,0,2,1:T(8,128)}), f32[48,1,2,256]{3,0,2,1:T(8,128)}) %all-reduce.12.cloned.1.call-update) | async-done | bytes 98320 | tf_op jit(solution)/shard_map/psum | solution.py:108
  187.2 18.1 %fusion = f32[8,448]{1,0:T(8,128)S(1)} fusion(f32[48,448]{1,0:T(8,128)S(1)} %fusion.35), kind=kCustom, calls=%all-reduce-scatter | all-reduce-scatter fusion | flops 28673 | bytes 101376
  205.3 3.4 collective-permute-start
  212.0 11.6 %psum.88 = f32[6]{0:T(128)S(1)} all-reduce(f32[6]{0:T(128)S(1)} %multiply_reduce_fusion.2), channel_id=1, replica_groups=mesh['kv'=8,'seq'=8,'vocab'=4] {'seq'}, use_global_device_ids=true, to_apply=%region_12.13 | all-reduce | flops 6 | bytes 48 | tf_op jit(solution)/shard_map/psum | solution.py:36
  223.7 20.5 %all_to_all.5 = bf16[32,6,448]{2,1,0:T(8,128)(2,1)S(1)} all-to-all(bf16[32,6,448]{2,1,0:T(8,128)(2,1)S(1)} %stack.20), channel_id=1, replica_groups=mesh['kv'=8,'seq'=8,'vocab'=4] {'kv','vocab'}, dimensions={0} | all-to-all | bytes 344064 | tf_op jit(solution)/shard_map/all_to_all | solution.py:137
  246.0 11.9 %psum.90 = f32[192]{0:T(256)S(1)} all-reduce(f32[192]{0:T(256)S(1)} %reduce_sum.187), channel_id=1, replica_groups=mesh['kv'=8,'seq'=8,'vocab'=4] {'seq'}, use_global_device_ids=true, to_apply=%region_15.16 | all-reduce | flops 192 | bytes 1536 | tf_op jit(solution)/shard_map/psum | solution.py:148
  257.9 53.8 %all-reduce.14.cloned.1.call-done = f32[192,2,448]{2,0,1:T(8,128)} async-done(((f32[192,2,448]{2,0,1:T(8,128)}), f32[192,2,448]{2,0,1:T(8,128)}) %all-reduce.14.cloned.1.call-update) | async-done | bytes 688144 | tf_op jit(solution)/shard_map/psum | solution.py:148
  313.3 68.1 %fusion.1 = f32[8,448]{1,0:T(8,128)S(1)} fusion(f32[192,448]{1,0:T(8,128)S(1)} %fusion.53), kind=kCustom, calls=%all-reduce-scatter.1 | all-reduce-scatter fusion | flops 114689 | bytes 359424
  383.3 1.9 collective-permute-start.3
  386.7 1.9 collective-permute-start.4
  390.5 5.9 collective-permute-start.6
  396.4 6.8 collective-permute-start.7
  403.3 3.9 collective-permute-start.8
  409.4 12.6 %psum.91 = f32[6]{0:T(128)S(1)} all-reduce(f32[6]{0:T(128)S(1)} %multiply_reduce_fusion.1), channel_id=1, replica_groups=mesh['kv'=8,'seq'=8,'vocab'=4] {'seq'}, use_global_device_ids=true, to_apply=%region_18.19 | all-reduce | flops 6 | bytes 48 | tf_op jit(solution)/shard_map/psum | solution.py:36
  422.3 10.7 %psum.92 = f32[6]{0:T(128)S(1)} all-reduce(f32[6]{0:T(128)S(1)} %get-tuple-element.17), channel_id=1, replica_groups=mesh['kv'=8,'seq'=8,'vocab'=4] {'seq'}, use_global_device_ids=true, to_apply=%region_20.21 | all-reduce | flops 6 | bytes 48 | tf_op jit(solution)/shard_map/psum | solution.py:36
  433.1 48.2 %all-gather.1 = bf16[32,6,448]{2,1,0:T(8,128)(2,1)S(1)} all-gather(bf16[1,6,448]{2,1,0:T(8,128)(2,1)S(1)} %fusion.82), channel_id=1, replica_groups=mesh['kv'=8,'seq'=8,'vocab'=4] {'kv','vocab'}, dimensions={0}, use_global_device_ids=true | all-gather | bytes 177408 | tf_op jit(solution)/shard_map/all_gather | solution.py:162
  483.5 64.1 %all-reduce.16.cloned.1.call-done = bf16[192,4,112]{2,0,1:T(8,128)(2,1)} async-done(((bf16[192,4,112]{2,0,1:T(8,128)(2,1)}), bf16[192,4,112]{2,0,1:T(8,128)(2,1)}) %all-reduce.16.cloned.1.call-update) | async-done | bytes 172048 | tf_op jit(solution)/shard_map/psum | solution.py:164
  553.7 2.5 fusion.6
  557.8 30.5 %all-gather.8.cloned.1.call-done = bf16[8,448,192]{1,2,0:T(8,128)(2,1)} async-done(((bf16[1,448,192]{1,2,0:T(8,128)(2,1)}), bf16[8,448,192]{1,2,0:T(8,128)(2,1)}) %all-gather.8.cloned.1.call-update) | async-done | bytes 1376272 | tf_op jit(solution)/shard_map/all_gather | solution.py:171
  588.3 2.3 copy.59
  590.6 2.7 reshape.417
  593.3 3.8 fusion.95
  597.2 52.4 %all-gather.6.cloned.1.call-done = bf16[192,4,3584]{0,1,2:T(4,128)(2,1)} async-done(((bf16[192,4,112]{0,1,2:T(4,128)(2,1)}), bf16[192,4,3584]{0,1,2:T(4,128)(2,1)}) %all-gather.6.cloned.1.call-update) | async-done | bytes 5505040 | tf_op jit(solution)/shard_map/all_gather | solution.py:179
  649.5 8.2 %fusion.17 = f32[192,4,512]{2,0,1:T(8,128)S(1)} fusion(bf16[512,3584]{1,0:T(8,128)(2,1)} %param.36, bf16[192,4,3584]{0,1,2:T(4,128)(2,1)} %all-gather.6.cloned.1.call-done, f32[192,512]{1,0:T(8,128)S(1)} %fusion.95), kind=kOutput, calls=%fused_computation.38 | convolution fusion | flops 2818965504 | bytes 11141120 | tf_op jit(solution)/shard_map/tnc,vc->tnv/dot_general | solution.py:177
  657.8 4.4 select_reduce_fusion
  663.6 76.6 %all-reduce.4 = (f32[192,5]{0,1:T(8,128)S(1)}, f32[5,48,4,8]{1,3,2,0:T(8,128)}) all-reduce(f32[192,5]{0,1:T(8,128)S(1)} %get-tuple-element.19, f32[5,48,4,8]{1,3,2,0:T(8,128)S(1)} %reshape.407), channel_id=1, replica_groups=mesh['kv'=8,'seq'=8,'vocab'=4] {'kv','seq','vocab'}, use_global_device_ids=true, to_apply=%region_23.24 | all-reduce | flops 8640 | bytes 69120 | tf_op jit(solution)/shard_map/psum | solution.py:205
  (152 shorter events, 32.2 us)
Async XLA Ops:
  7.2 237.2 %copy-start = (bf16[448,2,448]{2,1,0:T(2,128)(2,1)S(1)}, bf16[448,2,448]{2,1,0:T(2,128)(2,1)}, u32[]{:S(2)}) copy-start(bf16[448,2,448]{2,1,0:T(2,128)(2,1)} %param.32) | copy-start | bytes 2408452
  7.2 88.7 %copy-start.2 = (bf16[1,2048,1,256]{3,1,2,0:T(8,128)(2,1)S(1)}, bf16[1,2048,1,256]{3,1,2,0:T(8,128)(2,1)}, u32[]{:S(2)}) copy-start(bf16[1,2048,1,256]{3,1,2,0:T(8,128)(2,1)} %param.27) | copy-start | bytes 3145732
  7.2 87.3 %all-reduce.10.cloned.1.call-start = ((), (), s32[]{:S(2)}) async-start(), calls=%async_computation.1 | async-start | bytes 393216 | tf_op jit(solution)/shard_map/psum | solution.py:79
  26.1 83.6 %copy-start.1 = (bf16[1,2048,1,256]{3,1,2,0:T(8,128)(2,1)S(1)}, bf16[1,2048,1,256]{3,1,2,0:T(8,128)(2,1)}, u32[]{:S(2)}) copy-start(bf16[1,2048,1,256]{3,1,2,0:T(8,128)(2,1)} %param.28) | copy-start | bytes 3145732
  26.2 159.7 %all-reduce.12.cloned.1.call-start = ((), (), s32[]{:S(2)}) async-start(), calls=%async_computation.2 | async-start | bytes 196608 | tf_op jit(solution)/shard_map/psum | solution.py:108
  97.1 89.9 %copy-start.3 = (bf16[1,512,448]{1,2,0:T(8,128)(2,1)S(1)}, bf16[1,512,448]{1,2,0:T(8,128)(2,1)}, u32[]{:S(2)}) copy-start(bf16[1,512,448]{1,2,0:T(8,128)(2,1)} %param.21) | copy-start | bytes 1376260
  97.1 113.3 %copy-start.20 = (u32[256]{0:T(256)S(1)}, u32[256]{0:T(256)}, u32[]{:S(2)}) copy-start(u32[256]{0:T(256)} %constant.87) | copy-start | bytes 3076
  97.1 126.5 %copy-start.13 = (bf16[6,1,448]{2,0,1:T(8,128)(2,1)S(1)}, bf16[6,1,448]{2,0,1:T(8,128)(2,1)}, u32[]{:S(2)}) copy-start(bf16[6,1,448]{2,0,1:T(8,128)(2,1)} %param.19) | copy-start | bytes 16132
  97.1 126.5 %copy-start.16 = (f32[448]{0:T(512)S(1)}, f32[448]{0:T(512)}, u32[]{:S(2)}) copy-start(f32[448]{0:T(512)} %param.23) | copy-start | bytes 5380
  111.7 132.6 %copy-start.14 = (f32[448]{0:T(512)S(1)}, f32[448]{0:T(512)}, u32[]{:S(2)}) copy-start(f32[448]{0:T(512)} %param.24) | copy-start | bytes 5380
  111.7 199.9 %all-reduce.14.cloned.1.call-start = ((), (), s32[]{:S(2)}) async-start(), calls=%async_computation.3 | async-start | bytes 1572864 | tf_op jit(solution)/shard_map/psum | solution.py:148
  205.3 6.3 collective-permute-start
  208.8 2.8 collective-permute-start.1
  245.6 161.6 %copy-start.19 = (u32[256]{0:T(256)S(1)}, u32[256]{0:T(256)}, u32[]{:S(2)}) copy-start(u32[256]{0:T(256)} %constant.91) | copy-start | bytes 3076
  245.6 176.5 %copy-start.17 = (f32[448]{0:T(512)S(1)}, f32[448]{0:T(512)}, u32[]{:S(2)}) copy-start(f32[448]{0:T(512)} %param.25) | copy-start | bytes 5380
  245.6 187.4 %copy-start.18 = (f32[448]{0:T(512)S(1)}, f32[448]{0:T(512)}, u32[]{:S(2)}) copy-start(f32[448]{0:T(512)} %param.26) | copy-start | bytes 5380
  245.6 235.7 %copy-start.4 = (bf16[4,448,112]{2,1,0:T(8,128)(2,1)S(1)}, bf16[4,448,112]{2,1,0:T(8,128)(2,1)}, u32[]{:S(2)}) copy-start(bf16[4,448,112]{2,1,0:T(8,128)(2,1)} %param.34) | copy-start | bytes 1204228
  245.7 301.9 %all-reduce.16.cloned.1.call-start = ((), (), s32[]{:S(2)}) async-start(), calls=%async_computation.4 | async-start | bytes 393216 | tf_op jit(solution)/shard_map/psum | solution.py:164
  313.3 234.2 %copy-start.15 = (f32[4,112]{1,0:T(4,128)S(1)}, f32[4,112]{1,0:T(4,128)}, u32[]{:S(2)}) copy-start(f32[4,112]{1,0:T(4,128)} %param.35) | copy-start | bytes 5380
  381.4 15.1 %collective-permute-start.2 = (f32[8,448]{1,0:T(8,128)S(1)}, f32[8,448]{1,0:T(8,128)S(1)}, u32[]{:S(2)}, u32[]{:S(2)}) collective-permute-start(f32[8,448]{1,0:T(8,128)S(1)} %fusion.1), channel_id=1, source_target_pairs={{0,1},{1,2},{2,3},{3,32},{32,33},{33,34},{34,35},{35,64},{64,65},{... | collective-permute-start | bytes 43016
  383.3 20.0 %collective-permute-start.3 = (f32[8,448]{1,0:T(8,128)S(1)}, f32[8,448]{1,0:T(8,128)S(1)}, u32[]{:S(2)}, u32[]{:S(2)}) collective-permute-start(f32[8,448]{1,0:T(8,128)S(1)} %fusion.1), channel_id=1, source_target_pairs={{0,2},{1,3},{2,32},{3,33},{32,34},{33,35},{34,64},{35,65},{64,66},... | collective-permute-start | bytes 43016
  385.2 164.3 %copy-start.5 = (s32[5,48,4,8]{1,3,2,0:T(8,128)S(1)}, s32[5,48,4,8]{1,3,2,0:T(8,128)}, u32[]{:S(2)}) copy-start(s32[5,48,4,8]{1,3,2,0:T(8,128)} %param.37) | copy-start | bytes 92164
  385.2 5.3 collective-permute-start.9
  386.7 21.8 %collective-permute-start.4 = (f32[8,448]{1,0:T(8,128)S(1)}, f32[8,448]{1,0:T(8,128)S(1)}, u32[]{:S(2)}, u32[]{:S(2)}) collective-permute-start(f32[8,448]{1,0:T(8,128)S(1)} %fusion.1), channel_id=1, source_target_pairs={{0,3},{1,32},{2,33},{3,34},{32,35},{33,64},{34,65},{35,66},{64,67}... | collective-permute-start | bytes 43016
  388.6 19.9 %collective-permute-start.5 = (f32[8,448]{1,0:T(8,128)S(1)}, f32[8,448]{1,0:T(8,128)S(1)}, u32[]{:S(2)}, u32[]{:S(2)}) collective-permute-start(f32[8,448]{1,0:T(8,128)S(1)} %fusion.1), channel_id=1, source_target_pairs={{0,32},{1,33},{2,34},{3,35},{32,64},{33,65},{34,66},{35,67},{64,96... | collective-permute-start | bytes 43016
  390.5 17.9 %collective-permute-start.6 = (f32[8,448]{1,0:T(8,128)S(1)}, f32[8,448]{1,0:T(8,128)S(1)}, u32[]{:S(2)}, u32[]{:S(2)}) collective-permute-start(f32[8,448]{1,0:T(8,128)S(1)} %fusion.1), channel_id=1, source_target_pairs={{0,33},{1,34},{2,35},{3,64},{32,65},{33,66},{34,67},{35,96},{64,97... | collective-permute-start | bytes 43016
  396.4 12.1 %collective-permute-start.7 = (f32[8,448]{1,0:T(8,128)S(1)}, f32[8,448]{1,0:T(8,128)S(1)}, u32[]{:S(2)}, u32[]{:S(2)}) collective-permute-start(f32[8,448]{1,0:T(8,128)S(1)} %fusion.1), channel_id=1, source_target_pairs={{0,34},{1,35},{2,64},{3,65},{32,66},{33,67},{34,96},{35,97},{64,98... | collective-permute-start | bytes 43016
  403.3 5.2 collective-permute-start.8
  482.3 106.0 %all-gather.8.cloned.1.call-start = ((), (), s32[]{:S(2)}) async-start(), calls=%async_computation.6 | async-start | bytes 1769472 | tf_op jit(solution)/shard_map/all_gather | solution.py:171
  483.2 67.6 %copy-start.21 = (s32[1,5]{1,0:T(1,128)S(1)}, s32[1,5]{1,0:T(1,128)}, u32[]{:S(2)}) copy-start(s32[1,5]{1,0:T(1,128)} %param.31) | copy-start | bytes 64
  483.2 166.3 %all-gather.6.cloned.1.call-start = ((), (), s32[]{:S(2)}) async-start(), calls=%async_computation.5 | async-start | bytes 7569408 | tf_op jit(solution)/shard_map/all_gather | solution.py:179
  597.1 60.7 %copy-start.6 = (s32[192,5]{0,1:T(8,128)S(1)}, s32[192,5]{0,1:T(8,128)}, u32[]{:S(2)}) copy-start(s32[192,5]{0,1:T(8,128)} %get-tuple-element.43) | copy-start | bytes 11524
  (6 other events, 364.0 us)
Sparse Core Ops, SparseCore 0:
  26.3 68.1 all-reduce.9
  111.9 73.9 all-reduce.11
  245.8 65.8 all-reduce.13
  482.5 65.0 all-reduce.15
  549.2 39.1 all-gather.7
  590.8 58.7 all-gather.5
